TPU v7x, 256 devices: a whole 4x4x8 slice. The times are simulated.
256 devices in a mesh: blk: 32 (over y, z), row: 8 (over x, core).
Axes of the slice: x: 4, y: 4, z: 8, core: 2. Of those that a mesh axis runs over, the one named last changes fastest.
Arguments:
- far_kernel: bfloat16 [256, 8, 512, 512], P('blk', None, 'row'), may hold values from -0.25 to 0.25
- near_kernel: bfloat16 [256, 2, 512, 512], P('blk', None, 'row'), may hold values from -0.25 to 0.25
- samples: bfloat16 [256, 512, 128], P('blk'), may hold values from -18 to 18
- far_target: int32 [256, 8], P('blk'), may hold values from 0 to 255, as said below
Outputs:
- basis_out: float32 [256, 512, 128], P('blk', 'row')
- coupling: float32 [256, 8, 128, 128], P('blk', None, 'row')
- parent_samples: float32 [128, 256, 128], P('blk', 'row')
Inputs may be any that keep to these rules, and one draw needn't show every extreme that they name: `far_target`: each row names 8 different target clusters; among the far blocks of the source clusters of one index of blk (rows 8 * g to 8 * g + 7), at most 4 name targets of any one index of blk (clusters 8 * h to 8 * h + 7), and exactly 4 for some such index.
All inputs are finite; a program needn't handle non-finite values.
Results may differ from a plain program's by a relative error of at most 0.02.
Values may be sent and summed in bfloat16 or wider, within the bound.
No kernel may reach another device: no remote copies, remote signals or barrier semaphores. Data moves between devices by JAX's collectives and lax.ppermute only.
A program may use at most 64 MiB of HBM per device.

v0:
```python
import jax
import jax.numpy as jnp
from jax import lax
from jax.sharding import PartitionSpec as P

ITERS = 12


def inverse_root(gram_mat, full_width):
    highest = lax.Precision.HIGHEST
    sample_cols = gram_mat.shape[-1]
    identity = jnp.eye(sample_cols, dtype=jnp.float32)
    mean_sq = jnp.trace(gram_mat, axis1=1, axis2=2) / (full_width * sample_cols) + 1e-06
    level_mat = gram_mat / (full_width * sample_cols * mean_sq)[:, None, None]
    root_mat = jnp.broadcast_to(identity, gram_mat.shape)
    for sweep_index in range(ITERS):
        step_mat = 1.5 * identity - 0.5 * jnp.matmul(root_mat, level_mat, precision=highest)
        level_mat = jnp.matmul(level_mat, step_mat, precision=highest)
        root_mat = jnp.matmul(step_mat, root_mat, precision=highest)
    return root_mat / jnp.sqrt(sample_cols * mean_sq)[:, None, None]


def per_device(far_kernel, near_kernel, samples, far_target):
    highest = lax.Precision.HIGHEST
    local_count, far_count, row_count, full_width = far_kernel.shape
    sample_cols = samples.shape[2]
    row_offset = lax.axis_index("row") * row_count
    targets = far_target.reshape(local_count * far_count)
    flat_width = row_count * sample_cols
    products = jnp.einsum("cfrw,cws->cfrs", far_kernel, samples, preferred_element_type=jnp.float32)
    products = products.astype(jnp.bfloat16).reshape(local_count * far_count, flat_width)
    target_ids = lax.iota(jnp.int32, local_count * lax.axis_size("blk"))
    onehot = (target_ids[:, None] == targets[None, :]).astype(jnp.bfloat16)
    far_sketch = lax.psum_scatter(
        jnp.dot(onehot, products, preferred_element_type=jnp.float32).astype(jnp.bfloat16),
        "blk",
        scatter_dimension=0,
        tiled=True,
    ).astype(jnp.float32)
    sibling = samples.reshape(local_count // 2, 2, full_width, sample_cols)[:, ::-1].reshape(
        local_count, full_width, sample_cols
    )
    paired = jnp.stack([samples, sibling], axis=1)
    near_sum = jnp.einsum("ckrw,ckws->crs", near_kernel, paired, preferred_element_type=jnp.float32)
    sketch = far_sketch.reshape(local_count, row_count, sample_cols) - near_sum
    gram_part = jnp.einsum("crs,crt->cst", sketch, sketch, precision=highest)
    gram_mat = lax.psum(gram_part, "row")
    root_mat = inverse_root(gram_mat, full_width)
    basis_out = jnp.einsum("crs,cst->crt", sketch, root_mat, precision=highest)
    basis_half = basis_out.astype(jnp.bfloat16)
    start_sum = jnp.zeros((local_count, far_count, row_count, sample_cols), jnp.float32)
    segment = lax.all_gather(basis_half, "row", axis=1, tiled=True)
    columns = lax.slice_in_dim(far_kernel, 0, segment.shape[1], axis=3)
    mixed_rows = (
        start_sum
        + jnp.einsum("cfrw,cws->cfrs", columns, segment, preferred_element_type=jnp.float32)
    ).astype(jnp.bfloat16)
    basis_every = lax.all_gather(basis_half, "blk", axis=0, tiled=True)
    picked = jnp.take(basis_every, targets, axis=0).reshape(
        local_count, far_count, row_count, sample_cols
    )
    scale_root = jnp.sqrt(jnp.float32(full_width))
    own_samples = lax.dynamic_slice_in_dim(samples, row_offset, row_count, 1)
    parent_part = (
        jnp.einsum("crs,crt->cst", basis_half, own_samples, preferred_element_type=jnp.float32)
        / scale_root
    )
    parent_part = parent_part.reshape(local_count // 2, 2 * sample_cols, sample_cols)
    coupling_part = (
        jnp.einsum("cfrs,cfrt->cfst", picked, mixed_rows, preferred_element_type=jnp.float32)
        / scale_root
    )
    coupling, parent_samples = (
        lax.psum_scatter(coupling_part, "row", scatter_dimension=2, tiled=True),
        lax.psum_scatter(parent_part, "row", scatter_dimension=1, tiled=True),
    )
    return (basis_out, coupling, parent_samples)


def solution(mesh):
    return jax.shard_map(
        per_device,
        mesh=mesh,
        in_specs=(
            P("blk", None, "row", None),
            P("blk", None, "row", None),
            P("blk", None, None),
            P("blk", None),
        ),
        out_specs=(P("blk", "row", None), P("blk", None, "row", None), P("blk", "row", None)),
        check_vma=False,
    )
```

profile of v0, /device:TPU:8, one launch (start us, length us, event | category | flops | bytes accessed | tf_op | source)
XLA Modules:
  0.0 529.5 jit_solution(16602669929706069161)
XLA Ops:
  7.2 0.8 eq.53
  8.1 3.7 fusion.4
  11.8 3.2 convolution_convert_fusion
  15.2 225.7 %reduce-scatter.4.cloned.1.call-done = bf16[8,8192]{1,0:T(8,128)(2,1)} async-done(((bf16[256,8192]{1,0:T(8,128)(2,1)}), bf16[8,8192]{1,0:T(8,128)(2,1)}) %reduce-scatter.4.cloned.1.call-update) | async-done | bytes 131088 | tf_op jit(solution)/shard_map/reduce_scatter | solution.py:34
  240.9 0.9 bitcast_convert_fusion
  242.4 1.8 fusion.45
  244.5 65.0 %all-reduce.2.cloned.1.call-done = f32[8,128,128]{2,1,0:T(8,128)} async-done(((f32[8,128,128]{2,1,0:T(8,128)}), f32[8,128,128]{2,1,0:T(8,128)}) %all-reduce.2.cloned.1.call-update) | async-done | bytes 524304 | tf_op jit(solution)/shard_map/psum | solution.py:47
  309.5 1.2 select_reduce_fusion
  310.7 1.7 fusion.17
  313.0 1.7 fusion.36
  314.7 0.6 fusion.16
  315.4 0.6 fusion.47
  316.0 0.6 fusion.46
  316.7 0.6 fusion.15
  317.3 0.6 fusion.49
  318.0 0.6 fusion.48
  318.6 0.6 fusion.14
  319.3 0.6 fusion.51
  320.0 0.6 fusion.50
  320.6 0.6 fusion.13
  321.3 0.6 fusion.53
  321.9 0.6 fusion.52
  322.6 0.6 fusion.12
  323.2 0.6 fusion.55
  323.9 0.9 fusion.54
  324.8 0.6 fusion.11
  325.4 0.6 fusion.57
  326.7 0.6 fusion.10
  327.4 0.6 fusion.59
  328.0 0.6 fusion.58
  328.7 0.6 fusion.9
  329.4 0.6 fusion.61
  330.0 0.6 fusion.60
  330.7 0.6 fusion.8
  331.3 0.6 fusion.63
  332.0 0.6 fusion.62
  332.6 0.6 fusion.7
  334.0 0.6 fusion.65
  334.6 0.6 fusion.6
  335.3 0.6 convolution_divide_fusion
  335.9 1.6 fusion.44
  338.3 2.0 convolution_multiply_fusion.1
  340.4 77.0 %all-gather.3.cloned.1.call-done = bf16[256,64,128]{2,1,0:T(8,128)(2,1)} async-done(((bf16[8,64,128]{2,1,0:T(8,128)(2,1)}), bf16[256,64,128]{2,1,0:T(8,128)(2,1)}) %all-gather.3.cloned.1.call-update) | async-done | bytes 4194320 | tf_op jit(solution)/shard_map/all_gather | solution.py:58
  417.4 2.9 gather_fusion
  420.4 23.2 %all-gather.5.cloned.1.call-done = bf16[8,512,128]{2,1,0:T(8,128)(2,1)} async-done(((bf16[8,64,128]{2,1,0:T(8,128)(2,1)}), bf16[8,512,128]{2,1,0:T(8,128)(2,1)}) %all-gather.5.cloned.1.call-update) | async-done | bytes 1048592 | tf_op jit(solution)/shard_map/all_gather | solution.py:52
  443.5 6.3 %convolution_multiply_fusion = f32[8,8,128,128]{3,2,1,0:T(8,128)} fusion(bf16[8,8,64,512]{3,2,1,0:T(8,128)(2,1)} %param.4, bf16[8,512,128]{2,1,0:T(8,128)(2,1)} %all-gather.5.cloned.1.call-done, bf16[8,8,64,128]{3,2,1,0:T(8,128)(2,1)S(1)} %bitcast.112, pred[8,8]{1,0:T(8,128)(4,1)S(1)} %compare_and_fusion), kind=kOutput, calls=%fused_computation.2 | convolution fusion | flops 673185792 | bytes 10485824 | tf_op jit(solution)/shard_map/cfrs,cfrt->cfst/dot_general | solution.py:70
  449.8 30.5 %reduce-scatter.8.cloned.1.call-done = f32[4,32,128]{2,1,0:T(8,128)} async-done(((f32[4,256,128]{2,1,0:T(8,128)}), f32[4,32,128]{2,1,0:T(8,128)}) %reduce-scatter.8.cloned.1.call-update) | async-done | bytes 65552 | tf_op jit(solution)/shard_map/reduce_scatter | solution.py:75
  480.3 42.4 %reduce-scatter.6.cloned.1.call-done = f32[8,8,16,128]{3,2,1,0:T(8,128)} async-done(((f32[8,8,128,128]{3,2,1,0:T(8,128)}), f32[8,8,16,128]{3,2,1,0:T(8,128)}) %reduce-scatter.6.cloned.1.call-update) | async-done | bytes 524304 | tf_op jit(solution)/shard_map/reduce_scatter | solution.py:74
  (31 shorter events, 3.7 us)
Async XLA Ops:
  7.2 234.6 %copy-start = (bf16[8,2,64,512]{3,2,1,0:T(8,128)(2,1)S(1)}, bf16[8,2,64,512]{3,2,1,0:T(8,128)(2,1)}, u32[]{:S(2)}) copy-start(bf16[8,2,64,512]{3,2,1,0:T(8,128)(2,1)} %param.5) | copy-start | bytes 3145732
  7.2 233.7 %reduce-scatter.4.cloned.1.call-start = ((), (), s32[]{:S(2)}) async-start(), calls=%async_computation.3 | async-start | bytes 4325376 | tf_op jit(solution)/shard_map/reduce_scatter | solution.py:34
  11.8 3.3 copy-start.1
  15.1 294.4 %all-reduce.2.cloned.1.call-start = ((), (), s32[]{:S(2)}) async-start(), calls=%async_computation.4 | async-start | bytes 1048576 | tf_op jit(solution)/shard_map/psum | solution.py:47
  244.2 173.2 %all-gather.3.cloned.1.call-start = ((), (), s32[]{:S(2)}) async-start(), calls=%async_computation.5 | async-start | bytes 4325376 | tf_op jit(solution)/shard_map/all_gather | solution.py:58
  333.3 4.9 copy-start.2
  337.5 106.0 %all-gather.5.cloned.1.call-start = ((), (), s32[]{:S(2)}) async-start(), calls=%async_computation.6 | async-start | bytes 1179648 | tf_op jit(solution)/shard_map/all_gather | solution.py:52
  338.1 142.2 %reduce-scatter.8.cloned.1.call-start = ((), (), s32[]{:S(2)}) async-start(), calls=%async_computation.8 | async-start | bytes 589824 | tf_op jit(solution)/shard_map/reduce_scatter | solution.py:75
  340.3 182.4 %reduce-scatter.6.cloned.1.call-start = ((), (), s32[]{:S(2)}) async-start(), calls=%async_computation.7 | async-start | bytes 4718592 | tf_op jit(solution)/shard_map/reduce_scatter | solution.py:74
Sparse Core Ops, SparseCore 0:
  15.2 225.6 reduce-scatter.3
  244.3 65.1 all-reduce.1
  337.7 79.6 all-gather.2
  419.7 23.8 all-gather.4
  446.5 33.7 reduce-scatter.7
  483.3 39.3 reduce-scatter.5
where the time goes:
time: 530 us
  waiting for transfers between devices  464 us (88%)
  matrix products  44.1 us (8%)
  between operations  14.5 us (3%)
    reduce_scatter x1, waiting for transfers between devices, per_device(): lax.psum_scatter(jnp.dot(onehot, products, preferred_element_type=jnp.flo...  226 us
    all_gather x1, waiting for transfers between devices, per_device(): basis_every = lax.all_gather(basis_half, 'blk', axis=0, tiled=True)  77 us
    psum x1, waiting for transfers between devices, per_device(): gram_mat = lax.psum(gram_part, 'row')  65 us
    reduce_scatter x1, waiting for transfers between devices, per_device(): lax.psum_scatter(coupling_part, 'row', scatter_dimension=2, tiled=True)  42.4 us
    reduce_scatter x1, waiting for transfers between devices, per_device(): lax.psum_scatter(parent_part, 'row', scatter_dimension=1, tiled=True)  30.5 us
    all_gather x1, waiting for transfers between devices, per_device(): segment = lax.all_gather(basis_half, 'row', axis=1, tiled=True)  23.2 us
  transfers between devices with their start and end apart: 6, of which 6 were waited for; matrix products, arithmetic and copies ran while one was open for 2% of the time, Pallas kernels for 0%

commit v1 on v0

--- a/solution.py
+++ b/solution.py
@@ -44,7 +44,8 @@
     near_sum = jnp.einsum("ckrw,ckws->crs", near_kernel, paired, preferred_element_type=jnp.float32)
     sketch = far_sketch.reshape(local_count, row_count, sample_cols) - near_sum
     gram_part = jnp.einsum("crs,crt->cst", sketch, sketch, precision=highest)
-    gram_mat = lax.psum(gram_part, "row")
+    pieces = lax.all_gather(gram_part, "row")
+    gram_mat = jnp.sum(pieces, axis=0)
     root_mat = inverse_root(gram_mat, full_width)
     basis_out = jnp.einsum("crs,cst->crt", sketch, root_mat, precision=highest)
     basis_half = basis_out.astype(jnp.bfloat16)

time: 530 us -> 498 us (0.940)
  waiting for transfers between devices: 464 us -> 434 us
    psum x1 -> x0, waiting for transfers between devices: 65 us -> none  [per_device(): gram_mat = lax.psum(gram_part, 'row')]
    all_gather x0 -> x1, waiting for transfers between devices: none -> 33.5 us  [per_device(): pieces = lax.all_gather(gram_part, 'row')]
where the time goes in v1:
time: 498 us
  waiting for transfers between devices  434 us (87%)
  matrix products  42 us (8%)
  between operations  14.5 us (3%)
    reduce_scatter x1, waiting for transfers between devices, per_device(): lax.psum_scatter(jnp.dot(onehot, products, preferred_element_type=jnp.flo...  226 us
    all_gather x1, waiting for transfers between devices, per_device(): basis_every = lax.all_gather(basis_half, 'blk', axis=0, tiled=True)  77.8 us
    reduce_scatter x1, waiting for transfers between devices, per_device(): lax.psum_scatter(coupling_part, 'row', scatter_dimension=2, tiled=True)  42.4 us
    all_gather x1, waiting for transfers between devices, per_device(): pieces = lax.all_gather(gram_part, 'row')  33.5 us
    reduce_scatter x1, waiting for transfers between devices, per_device(): lax.psum_scatter(parent_part, 'row', scatter_dimension=1, tiled=True)  30.5 us
    all_gather x1, waiting for transfers between devices, per_device(): segment = lax.all_gather(basis_half, 'row', axis=1, tiled=True)  23.2 us
  transfers between devices with their start and end apart: 6, of which 6 were waited for; matrix products, arithmetic and copies ran while one was open for 2% of the time, Pallas kernels for 0%

profile of v1, /device:TPU:8, one launch (start us, length us, event | category | flops | bytes accessed | tf_op | source)
XLA Modules:
  0.0 498.2 jit_solution(11571268331857569269)
XLA Ops:
  7.2 0.8 eq.53
  8.1 3.7 fusion.4
  11.8 3.2 convolution_convert_fusion
  15.2 225.7 %reduce-scatter.4.cloned.1.call-done = bf16[8,8192]{1,0:T(8,128)(2,1)} async-done(((bf16[256,8192]{1,0:T(8,128)(2,1)}), bf16[8,8192]{1,0:T(8,128)(2,1)}) %reduce-scatter.4.cloned.1.call-update) | async-done | bytes 131088 | tf_op jit(solution)/shard_map/reduce_scatter | solution.py:34
  240.9 0.9 bitcast_convert_fusion
  242.4 1.8 fusion.45
  244.5 33.5 %all-gather.9.cloned.1.call-done = f32[64,128,128]{2,1,0:T(8,128)} async-done(((f32[8,128,128]{2,1,0:T(8,128)}), f32[64,128,128]{2,1,0:T(8,128)}) %all-gather.9.cloned.1.call-update) | async-done | bytes 4194320 | tf_op jit(solution)/shard_map/all_gather | solution.py:47
  277.9 2.5 reduce_sum.19
  280.6 0.7 fusion.17
  281.3 0.7 fusion.36
  282.6 0.6 fusion.16
  283.2 0.6 fusion.47
  283.9 0.6 fusion.46
  284.5 0.6 fusion.15
  285.2 0.6 fusion.49
  285.8 0.6 fusion.48
  286.5 0.6 fusion.14
  287.2 0.6 fusion.51
  287.8 0.6 fusion.50
  288.5 0.6 fusion.13
  289.1 0.6 fusion.53
  289.8 0.6 fusion.52
  290.4 0.6 fusion.12
  291.1 0.6 fusion.55
  291.7 0.9 fusion.54
  292.6 0.6 fusion.11
  293.9 0.6 fusion.56
  294.6 0.6 fusion.10
  295.2 0.6 fusion.59
  296.5 0.6 fusion.9
  297.2 0.6 fusion.61
  297.9 0.6 fusion.60
  298.5 0.6 fusion.8
  299.2 0.6 fusion.63
  299.8 0.6 fusion.62
  300.5 0.6 fusion.7
  301.1 0.6 fusion.64
  301.8 0.6 fusion.65
  302.5 0.6 fusion.6
  303.1 0.6 convolution_divide_fusion
  303.8 1.6 fusion.44
  306.1 2.0 convolution_multiply_fusion.1
  308.2 77.8 %all-gather.5.cloned.1.call-done = bf16[256,64,128]{2,1,0:T(8,128)(2,1)} async-done(((bf16[8,64,128]{2,1,0:T(8,128)(2,1)}), bf16[256,64,128]{2,1,0:T(8,128)(2,1)}) %all-gather.5.cloned.1.call-update) | async-done | bytes 4194320 | tf_op jit(solution)/shard_map/all_gather | solution.py:59
  386.0 2.9 gather_fusion
  389.0 23.2 %all-gather.7.cloned.1.call-done = bf16[8,512,128]{2,1,0:T(8,128)(2,1)} async-done(((bf16[8,64,128]{2,1,0:T(8,128)(2,1)}), bf16[8,512,128]{2,1,0:T(8,128)(2,1)}) %all-gather.7.cloned.1.call-update) | async-done | bytes 1048592 | tf_op jit(solution)/shard_map/all_gather | solution.py:53
  412.2 6.3 %convolution_multiply_fusion = f32[8,8,128,128]{3,2,1,0:T(8,128)} fusion(bf16[8,8,64,512]{3,2,1,0:T(8,128)(2,1)} %param.4, bf16[8,512,128]{2,1,0:T(8,128)(2,1)} %all-gather.7.cloned.1.call-done, bf16[8,8,64,128]{3,2,1,0:T(8,128)(2,1)S(1)} %bitcast.114, pred[8,8]{1,0:T(8,128)(4,1)S(1)} %compare_and_fusion), kind=kOutput, calls=%fused_computation.2 | convolution fusion | flops 673185792 | bytes 10485824 | tf_op jit(solution)/shard_map/cfrs,cfrt->cfst/dot_general | solution.py:71
  418.4 30.5 %reduce-scatter.8.cloned.1.call-done = f32[4,32,128]{2,1,0:T(8,128)} async-done(((f32[4,256,128]{2,1,0:T(8,128)}), f32[4,32,128]{2,1,0:T(8,128)}) %reduce-scatter.8.cloned.1.call-update) | async-done | bytes 65552 | tf_op jit(solution)/shard_map/reduce_scatter | solution.py:76
  448.9 42.4 %reduce-scatter.6.cloned.1.call-done = f32[8,8,16,128]{3,2,1,0:T(8,128)} async-done(((f32[8,8,128,128]{3,2,1,0:T(8,128)}), f32[8,8,16,128]{3,2,1,0:T(8,128)}) %reduce-scatter.6.cloned.1.call-update) | async-done | bytes 524304 | tf_op jit(solution)/shard_map/reduce_scatter | solution.py:75
  (32 shorter events, 3.8 us)
Async XLA Ops:
  7.2 234.6 %copy-start = (bf16[8,2,64,512]{3,2,1,0:T(8,128)(2,1)S(1)}, bf16[8,2,64,512]{3,2,1,0:T(8,128)(2,1)}, u32[]{:S(2)}) copy-start(bf16[8,2,64,512]{3,2,1,0:T(8,128)(2,1)} %param.5) | copy-start | bytes 3145732
  7.2 233.7 %reduce-scatter.4.cloned.1.call-start = ((), (), s32[]{:S(2)}) async-start(), calls=%async_computation.3 | async-start | bytes 4325376 | tf_op jit(solution)/shard_map/reduce_scatter | solution.py:34
  11.8 3.3 copy-start.1
  15.1 262.9 %all-gather.9.cloned.1.call-start = ((), (), s32[]{:S(2)}) async-start(), calls=%async_computation.8 | async-start | bytes 4718592 | tf_op jit(solution)/shard_map/all_gather | solution.py:47
  244.2 141.9 %all-gather.5.cloned.1.call-start = ((), (), s32[]{:S(2)}) async-start(), calls=%async_computation.4 | async-start | bytes 4325376 | tf_op jit(solution)/shard_map/all_gather | solution.py:59
  301.1 4.9 copy-start.2
  305.4 106.8 %all-gather.7.cloned.1.call-start = ((), (), s32[]{:S(2)}) async-start(), calls=%async_computation.5 | async-start | bytes 1179648 | tf_op jit(solution)/shard_map/all_gather | solution.py:53
  306.0 143.0 %reduce-scatter.8.cloned.1.call-start = ((), (), s32[]{:S(2)}) async-start(), calls=%async_computation.7 | async-start | bytes 589824 | tf_op jit(solution)/shard_map/reduce_scatter | solution.py:76
  308.1 183.2 %reduce-scatter.6.cloned.1.call-start = ((), (), s32[]{:S(2)}) async-start(), calls=%async_computation.6 | async-start | bytes 4718592 | tf_op jit(solution)/shard_map/reduce_scatter | solution.py:75
Sparse Core Ops, SparseCore 0:
  15.2 225.6 reduce-scatter.3
  244.3 33.6 all-gather.8
  305.5 80.4 all-gather.4
  388.3 23.8 all-gather.6
  415.1 33.7 reduce-scatter.7
  451.9 39.3 reduce-scatter.5
